TPU v7x, 32 devices: a whole 2x2x4 slice. The times are simulated.
32 devices in a mesh: grp: 4 (over z), band: 8 (over y, x, core).
Axes of the slice: x: 2, y: 2, z: 4, core: 2. Of those that a mesh axis runs over, the one named last changes fastest.
Arguments:
- latent: bfloat16 [16384, 512], P(('grp', 'band')), may hold values from -6 to 6
- obs_feat: bfloat16 [4096, 512], P(('grp', 'band')), may hold values from -6 to 6
- obs_bias: bfloat16 [4096], P(('grp', 'band')), may hold values from -240 to 240
- obs_route: int32 [512, 1], P(('grp', 'band')), may hold values from 0 to 7; in each aligned block of 16 rows (0 to 15, 16 to 31, ...) at most 2 rows name the same one
- obs_tile_mask: int32 [512, 8], P(('grp', 'band')), may hold values 0 or 1
- w_query: bfloat16 [512, 512], replicated, may hold values from -0.25 to 0.25
- w_key: bfloat16 [512, 512], replicated, may hold values from -0.25 to 0.25
- w_value: bfloat16 [512, 512], replicated, may hold values from -0.25 to 0.25
- w_out: bfloat16 [512, 512], replicated, may hold values from -0.25 to 0.25
- grad_out: bfloat16 [16384, 512], P(('grp', 'band')), may hold values from -6 to 6
Outputs:
- attended: bfloat16 [16384, 512], P(('grp', 'band'))
- grad_latent: bfloat16 [16384, 512], P(('grp', 'band'))
- grad_obs: bfloat16 [4096, 512], P(('grp', 'band'))
- grad_weights: float32 [2048, 512], P('band')
Inputs may be any that keep to these rules, and one draw needn't show every extreme that they name: `obs_route`: among the 16 blocks of one device no band is named more than 2 times, a bound that some block reaches by some device in every draw.
All inputs are finite; a program needn't handle non-finite values. No bound on the sum of `obs_tile_mask` on one device may be relied on, other than what follows from the above.
Results may differ from a plain program's by a relative error of at most 0.023.
Values may be sent and summed in bfloat16 or wider, within the bound.
A program may use at most 64 MiB of HBM per device.

v0:
```python
import math
import jax
import jax.numpy as jnp
from jax import lax
from jax.sharding import PartitionSpec as P

HEADS = 16
QTILE = 64
OB = 8
SRC_BLK = 16
CAP = 2


def band_attention(query, dattn, keys, values, key_bias, visible, head_size):
    scale = 1.0 / math.sqrt(head_size)
    lat_rows = query.shape[0]
    key_rows = keys.shape[0]
    group_width = 4 * head_size

    def per_group(index):
        start = index * group_width
        query_g = lax.dynamic_slice_in_dim(query, start, group_width, 1).reshape(
            lat_rows, 4, head_size
        )
        dattn_g = lax.dynamic_slice_in_dim(dattn, start, group_width, 1).reshape(
            lat_rows, 4, head_size
        )
        keys_g = lax.dynamic_slice_in_dim(keys, start, group_width, 1).reshape(
            key_rows, 4, head_size
        )
        values_g = lax.dynamic_slice_in_dim(values, start, group_width, 1).reshape(
            key_rows, 4, head_size
        )
        scores = (
            jnp.einsum("qhd,khd->hqk", query_g, keys_g, preferred_element_type=jnp.float32) * scale
            + key_bias[None, None, :]
        )
        masked = jnp.where(visible[None], scores, -jnp.inf)
        top = jnp.maximum(jnp.max(masked, axis=-1), 0.0)
        expo = jnp.where(visible[None], jnp.exp(scores - top[..., None]), 0.0)
        total = jnp.exp(-top) + jnp.sum(expo, axis=-1)
        prob = expo / total[..., None]
        prob_b = prob.astype(jnp.bfloat16)
        attn_g = jnp.einsum("hqk,khd->qhd", prob_b, values_g, preferred_element_type=jnp.float32)
        dprob = jnp.einsum("qhd,khd->hqk", dattn_g, values_g, preferred_element_type=jnp.float32)
        delta = jnp.sum(prob * dprob, axis=-1)
        dscore = (prob * (dprob - delta[..., None])).astype(jnp.bfloat16)
        dquery_g = (
            jnp.einsum("hqk,khd->qhd", dscore, keys_g, preferred_element_type=jnp.float32) * scale
        )
        dkeys_g = (
            jnp.einsum("hqk,qhd->khd", dscore, query_g, preferred_element_type=jnp.float32) * scale
        )
        dvalues_g = jnp.einsum("hqk,qhd->khd", prob_b, dattn_g, preferred_element_type=jnp.float32)
        return (
            attn_g.reshape(lat_rows, group_width).astype(jnp.bfloat16),
            dquery_g.reshape(lat_rows, group_width).astype(jnp.bfloat16),
            dkeys_g.reshape(key_rows, group_width).astype(jnp.bfloat16),
            dvalues_g.reshape(key_rows, group_width).astype(jnp.bfloat16),
        )

    groups = query.shape[1] // group_width
    stacked = lax.map(per_group, jnp.arange(groups))

    def unstack(piece):
        return jnp.transpose(piece, (1, 0, 2)).reshape(piece.shape[1], groups * group_width)

    return tuple((unstack(piece) for piece in stacked))


def per_device(
    latent, obs_feat, obs_bias, obs_route, obs_tile_mask, w_query, w_key, w_value, w_out, grad_out
):
    band_count = lax.axis_size("band")
    group_count = lax.axis_size("grp")
    slots = band_count * CAP
    lat_rows = latent.shape[0]
    width = latent.shape[1]
    head_size = width // HEADS
    tile_count = obs_tile_mask.shape[1]
    route = obs_route[:, 0]
    order = jnp.arange(SRC_BLK)
    earlier = order[:, None] < order[None, :]
    rank = jnp.sum(((route[:, None] == route[None, :]) & earlier).astype(jnp.int32), axis=0)
    position = route * CAP + rank
    placing = (jnp.arange(slots)[:, None] == position[None, :]).astype(jnp.bfloat16)
    send_bias = jnp.dot(
        placing, obs_bias.reshape(SRC_BLK, OB), preferred_element_type=jnp.float32
    ).astype(jnp.bfloat16)
    send_mask = jnp.dot(
        placing, obs_tile_mask.astype(jnp.bfloat16), preferred_element_type=jnp.float32
    ).astype(jnp.bfloat16)
    w_pair = jnp.concatenate([w_key, w_value], axis=1)
    send_feat = jnp.dot(
        placing, obs_feat.reshape(SRC_BLK, OB * width), preferred_element_type=jnp.float32
    ).astype(jnp.bfloat16)
    recv_feat, recv_bias, recv_mask = (
        lax.all_to_all(send_feat, "band", split_axis=0, concat_axis=0, tiled=True),
        lax.all_to_all(send_bias, "band", split_axis=0, concat_axis=0, tiled=True),
        lax.all_to_all(send_mask, "band", split_axis=0, concat_axis=0, tiled=True),
    )
    recv_rows = recv_feat.reshape(slots * OB, width)
    arrived = jnp.dot(recv_rows, w_pair, preferred_element_type=jnp.float32).astype(jnp.bfloat16)
    keys = arrived[:, :width]
    values = arrived[:, width:]
    key_bias = recv_bias.reshape(slots * OB).astype(jnp.float32)
    row_tile = jnp.arange(lat_rows) // QTILE
    tile_pick = (row_tile[:, None] == jnp.arange(tile_count)[None, :]).astype(jnp.bfloat16)
    slot_seen = jnp.dot(tile_pick, recv_mask.T, preferred_element_type=jnp.float32) > 0.5
    visible = jnp.broadcast_to(slot_seen[:, :, None], (lat_rows, slots, OB)).reshape(
        lat_rows, slots * OB
    )
    query = jnp.dot(latent, w_query, preferred_element_type=jnp.float32).astype(jnp.bfloat16)
    dattn = jnp.dot(grad_out, w_out.T, preferred_element_type=jnp.float32).astype(jnp.bfloat16)
    attn, dquery, dkeys, dvalues = band_attention(
        query, dattn, keys, values, key_bias, visible, head_size
    )
    attended = jnp.dot(attn, w_out, preferred_element_type=jnp.float32).astype(jnp.bfloat16)
    grad_latent = jnp.dot(dquery, w_query.T, preferred_element_type=jnp.float32).astype(
        jnp.bfloat16
    )
    dpair_slots = jnp.concatenate([dkeys, dvalues], axis=1)
    feat_grad = jnp.dot(dpair_slots, w_pair.T, preferred_element_type=jnp.float32).astype(
        jnp.bfloat16
    )
    returned = lax.all_to_all(
        feat_grad.reshape(slots, OB * width), "band", split_axis=0, concat_axis=0, tiled=True
    )
    grad_obs = (
        jnp.dot(placing.T, returned, preferred_element_type=jnp.float32)
        .astype(jnp.bfloat16)
        .reshape(SRC_BLK * OB, width)
    )
    grad_pair = jnp.einsum("ri,rj->ij", recv_rows, dpair_slots, preferred_element_type=jnp.float32)
    grad_wq = jnp.einsum("ri,rj->ij", latent, dquery, preferred_element_type=jnp.float32)
    grad_wo = jnp.einsum("ri,rj->ij", attn, grad_out, preferred_element_type=jnp.float32)
    term = jnp.concatenate(
        [grad_wq, grad_pair[:, :width], grad_pair[:, width:], grad_wo], axis=0
    ) / float(group_count)
    band_rows = lax.psum_scatter(term.astype(jnp.bfloat16), "band", scatter_dimension=0, tiled=True)
    grads = lax.psum(band_rows, "grp").astype(jnp.float32)
    return (attended, grad_latent, grad_obs, grads)


def solution(mesh):
    return jax.shard_map(
        per_device,
        mesh=mesh,
        in_specs=(
            P(("grp", "band"), None),
            P(("grp", "band"), None),
            P(("grp", "band")),
            P(("grp", "band"), None),
            P(("grp", "band"), None),
            P(),
            P(),
            P(),
            P(),
            P(("grp", "band"), None),
        ),
        out_specs=(
            P(("grp", "band"), None),
            P(("grp", "band"), None),
            P(("grp", "band"), None),
            P("band", None),
        ),
        check_vma=False,
    )
```

profile of v0, /device:TPU:0, one launch (start us, length us, event | category | flops | bytes accessed | tf_op | source)
XLA Modules:
  0.0 164.6 jit_solution(14191782597755601926)
XLA Ops:
  7.2 0.9 convert_reduce_fusion
  8.1 0.7 multiply_add_fusion
  8.7 0.7 reshape.147
  9.7 0.7 copy.38
  10.3 5.2 %all-to-all-start.2 = ((bf16[8,2,8]{2,1,0:T(2,128)(2,1)}), bf16[8,2,8]{2,1,0:T(2,128)(2,1)S(1)}, u32[]{:S(2)}, u32[]{:S(2)}) async-start(bf16[8,2,8]{2,1,0:T(2,128)(2,1)} %bitcast.1), calls=%async_computation.2 | async-start | bytes 8192 | tf_op jit(solution)/shard_map/all_to_all | solution.py:99
  15.6 1.0 reshape.145
  16.8 1.1 constant_dynamic-update-slice_fusion.5
  17.9 0.8 convolution_convert_fusion.10
  18.7 1.1 constant_dynamic-update-slice_fusion.4
  19.8 1.2 convolution_convert_fusion.7
  21.1 1.3 convolution_convert_fusion.6
  22.3 0.7 copy.39
  23.0 4.2 %all-to-all-start.1 = ((bf16[8,2,8]{2,1,0:T(2,128)(2,1)}), bf16[8,2,8]{2,1,0:T(2,128)(2,1)S(1)}, u32[]{:S(2)}, u32[]{:S(2)}) async-start(bf16[8,2,8]{2,1,0:T(2,128)(2,1)} %bitcast.2), calls=%async_computation.1 | async-start | bytes 8192 | tf_op jit(solution)/shard_map/all_to_all | solution.py:100
  27.2 0.8 all_to_all.28
  28.1 3.8 %all-to-all-done.1 = bf16[8,2,8]{2,1,0:T(2,128)(2,1)S(1)} async-done(((bf16[8,2,8]{2,1,0:T(2,128)(2,1)}), bf16[8,2,8]{2,1,0:T(2,128)(2,1)S(1)}, u32[]{:S(2)}, u32[]{:S(2)}) %all-to-all-start.1) | async-done | bytes 288 | tf_op jit(solution)/shard_map/all_to_all | solution.py:100
  31.9 3.4 %all-to-all-start = ((bf16[8,2,4096]{2,1,0:T(2,128)(2,1)}), bf16[8,2,4096]{2,1,0:T(2,128)(2,1)S(1)}, u32[]{:S(2)}, u32[]{:S(2)}) async-start(bf16[8,2,4096]{2,1,0:T(2,128)(2,1)} %all_to_all.28), calls=%async_computation | async-start | bytes 262144 | tf_op jit(solution)/shard_map/all_to_all | solution.py:98
  35.6 5.1 %all-to-all-done = bf16[8,2,4096]{2,1,0:T(2,128)(2,1)S(1)} async-done(((bf16[8,2,4096]{2,1,0:T(2,128)(2,1)}), bf16[8,2,4096]{2,1,0:T(2,128)(2,1)S(1)}, u32[]{:S(2)}, u32[]{:S(2)}) %all-to-all-start) | async-done | bytes 131104 | tf_op jit(solution)/shard_map/all_to_all | solution.py:98
  41.1 30.6 %while.17 = (s32[]{:T(128)}, bf16[4,512,128]{1,2,0:T(8,128)(2,1)}, bf16[4,512,128]{1,2,0:T(8,128)(2,1)}, bf16[4,128,128]{1,2,0:T(8,128)(2,1)}, bf16[4,128,128]{1...) while((s32[]{:T(128)}, bf16[4,512,128]{1,2,0:T(8,128)(2,1)}, ...), condition=%wide.region_5.6_spmd.clone, body=%wide.region_1.5_spmd.clone.sunk | while | flops 107726848 | bytes 13525743 | solution.py:63
  41.2 0.6 dynamic_slice.34
  42.5 0.9 constant_dynamic-slice_fusion.9
  43.5 0.4 select_reduce_fusion.2
  44.2 0.9 constant_dynamic-slice_fusion.10
  45.4 0.5 multiply_reduce_fusion.2
  46.4 0.4 convolution_convert_fusion.14
  46.8 0.7 constant_dynamic-update-slice_fusion.8
  48.1 0.7 constant_dynamic-update-slice_fusion.9
  48.8 0.6 dynamic_slice.34
  50.1 0.9 constant_dynamic-slice_fusion.9
  51.2 0.4 select_reduce_fusion.2
  51.8 0.9 constant_dynamic-slice_fusion.10
  53.0 0.5 multiply_reduce_fusion.2
  54.0 0.4 convolution_convert_fusion.14
  54.4 0.7 constant_dynamic-update-slice_fusion.8
  55.8 0.7 constant_dynamic-update-slice_fusion.9
  56.5 0.6 dynamic_slice.34
  57.8 0.9 constant_dynamic-slice_fusion.9
  58.8 0.4 select_reduce_fusion.2
  59.5 0.9 constant_dynamic-slice_fusion.10
  60.7 0.5 multiply_reduce_fusion.2
  61.7 0.4 convolution_convert_fusion.14
  62.1 0.7 constant_dynamic-update-slice_fusion.8
  63.5 0.7 constant_dynamic-update-slice_fusion.9
  64.1 0.6 dynamic_slice.34
  65.4 0.9 constant_dynamic-slice_fusion.9
  66.5 0.4 select_reduce_fusion.2
  67.2 0.9 constant_dynamic-slice_fusion.10
  68.3 0.5 multiply_reduce_fusion.2
  69.3 0.4 convolution_convert_fusion.14
  69.7 0.7 constant_dynamic-update-slice_fusion.8
  71.1 0.7 constant_dynamic-update-slice_fusion.9
  71.8 1.5 fusion.27
  73.3 0.5 fusion.12
  74.0 0.8 copy-done.4
  75.0 0.5 convolution_bitcast_fusion
  75.5 1.9 %fusion.11 = bf16[2048,512]{1,0:T(8,128)(2,1)} fusion(f32[512,512]{1,0:T(8,128)S(1)} %fusion.27, f32[512,512]{1,0:T(8,128)S(1)} %get-tuple-element.169, f32[512,512]{1,0:T(8,128)S(1)} %get-tuple-element.168, f32[512,512]{1,0:T(8,128)S(1)} %convolution_bitcast_fusion), kind=kLoop, calls=%fused_computation.31 | loop fusion | flops 5242880 | bytes 6291456 | tf_op jit(solution)/shard_map/convert_element_type | solution.py:140
  77.4 0.5 convolution_convert_fusion.9
  77.9 0.7 all_to_all.35
  78.6 3.4 %all-to-all-start.3 = ((bf16[8,2,4096]{2,1,0:T(2,128)(2,1)}), bf16[8,2,4096]{2,1,0:T(2,128)(2,1)S(1)}, u32[]{:S(2)}, u32[]{:S(2)}) async-start(bf16[8,2,4096]{2,1,0:T(2,128)(2,1)} %all_to_all.35), calls=%async_computation.3 | async-start | bytes 262144 | tf_op jit(solution)/shard_map/all_to_all | solution.py:126
  82.1 2.3 %convolution_convert_fusion.5 = bf16[512,512]{1,0:T(8,128)(2,1)} fusion(bf16[512,512]{0,1:T(8,128)(2,1)} %bitcast.123, bf16[512,512]{1,0:T(8,128)(2,1)S(1)} %copy-done.7), kind=kOutput, calls=%fused_computation.34 | convolution fusion | flops 268697600 | bytes 1572864 | tf_op jit(solution)/shard_map/dot_general | solution.py:118
  84.4 33.6 %reduce-scatter.2.cloned.1.call-done = bf16[256,512]{1,0:T(8,128)(2,1)} async-done(((bf16[2048,512]{1,0:T(8,128)(2,1)}), bf16[256,512]{1,0:T(8,128)(2,1)}) %reduce-scatter.2.cloned.1.call-update) | async-done | bytes 262160 | tf_op jit(solution)/shard_map/reduce_scatter | solution.py:140
  118.1 1.3 convolution_convert_fusion.4
  119.6 0.7 reshape.152
  120.4 35.6 %all-reduce.2.cloned.1.call-done = bf16[256,512]{1,0:T(8,128)(2,1)} async-done(((bf16[256,512]{1,0:T(8,128)(2,1)}), bf16[256,512]{1,0:T(8,128)(2,1)}) %all-reduce.2.cloned.1.call-update) | async-done | bytes 262160 | tf_op jit(solution)/shard_map/psum | solution.py:141
  155.9 1.8 %convert_element_type.135 = f32[256,512]{1,0:T(8,128)} convert(bf16[256,512]{1,0:T(8,128)(2,1)} %all-reduce.2.cloned.1.call-done) | non-fusion elementwise | flops 131072 | bytes 786432 | tf_op jit(solution)/shard_map/convert_element_type | solution.py:141
  (97 shorter events, 9.6 us)
Async XLA Ops:
  7.2 13.9 %copy-start = (bf16[512,512]{1,0:T(8,128)(2,1)S(1)}, bf16[512,512]{1,0:T(8,128)(2,1)}, u32[]{:S(2)}) copy-start(bf16[512,512]{1,0:T(8,128)(2,1)} %param.21) | copy-start | bytes 1572868
  7.2 12.6 %copy-start.3 = (bf16[512,512]{1,0:T(8,128)(2,1)S(1)}, bf16[512,512]{1,0:T(8,128)(2,1)}, u32[]{:S(2)}) copy-start(bf16[512,512]{1,0:T(8,128)(2,1)} %param.12) | copy-start | bytes 1572868
  7.2 12.6 %copy-start.1 = (bf16[512,512]{1,0:T(8,128)(2,1)S(1)}, bf16[512,512]{1,0:T(8,128)(2,1)}, u32[]{:S(2)}) copy-start(bf16[512,512]{1,0:T(8,128)(2,1)} %param.17) | copy-start | bytes 1572868
  10.3 12.7 %all-to-all-start.2 = ((bf16[8,2,8]{2,1,0:T(2,128)(2,1)}), bf16[8,2,8]{2,1,0:T(2,128)(2,1)S(1)}, u32[]{:S(2)}, u32[]{:S(2)}) async-start(bf16[8,2,8]{2,1,0:T(2,128)(2,1)} %bitcast.1), calls=%async_computation.2 | async-start | bytes 8192 | tf_op jit(solution)/shard_map/all_to_all | solution.py:99
  15.6 5.5 %copy-start.6 = (bf16[512,512]{1,0:T(8,128)(2,1)S(1)}, bf16[512,512]{1,0:T(8,128)(2,1)}, u32[]{:S(2)}) copy-start(bf16[512,512]{1,0:T(8,128)(2,1)} %param.20) | copy-start | bytes 1572868
  23.0 8.9 %all-to-all-start.1 = ((bf16[8,2,8]{2,1,0:T(2,128)(2,1)}), bf16[8,2,8]{2,1,0:T(2,128)(2,1)S(1)}, u32[]{:S(2)}, u32[]{:S(2)}) async-start(bf16[8,2,8]{2,1,0:T(2,128)(2,1)} %bitcast.2), calls=%async_computation.1 | async-start | bytes 8192 | tf_op jit(solution)/shard_map/all_to_all | solution.py:100
  31.9 8.8 %all-to-all-start = ((bf16[8,2,4096]{2,1,0:T(2,128)(2,1)}), bf16[8,2,4096]{2,1,0:T(2,128)(2,1)S(1)}, u32[]{:S(2)}, u32[]{:S(2)}) async-start(bf16[8,2,4096]{2,1,0:T(2,128)(2,1)} %all_to_all.28), calls=%async_computation | async-start | bytes 262144 | tf_op jit(solution)/shard_map/all_to_all | solution.py:98
  35.3 82.8 %reduce-scatter.2.cloned.1.call-start = ((), (), s32[]{:S(2)}) async-start(), calls=%async_computation.5 | async-start | bytes 2359296 | tf_op jit(solution)/shard_map/reduce_scatter | solution.py:140
  71.8 1.5 copy-start.8
  71.8 1.5 copy-start.9
  73.8 1.0 copy-start.4
  73.8 1.2 copy-start.5
  77.4 4.7 %copy-start.7 = (bf16[512,512]{1,0:T(8,128)(2,1)S(1)}, bf16[512,512]{1,0:T(8,128)(2,1)}, u32[]{:S(2)}) copy-start(bf16[512,512]{1,0:T(8,128)(2,1)} %param.20) | copy-start | bytes 1572868
  77.4 40.7 %copy-start.2 = (bf16[512,512]{1,0:T(8,128)(2,1)S(1)}, bf16[512,512]{1,0:T(8,128)(2,1)}, u32[]{:S(2)}) copy-start(bf16[512,512]{1,0:T(8,128)(2,1)} %param.17) | copy-start | bytes 1572868
  78.6 40.7 %all-to-all-start.3 = ((bf16[8,2,4096]{2,1,0:T(2,128)(2,1)}), bf16[8,2,4096]{2,1,0:T(2,128)(2,1)S(1)}, u32[]{:S(2)}, u32[]{:S(2)}) async-start(bf16[8,2,4096]{2,1,0:T(2,128)(2,1)} %all_to_all.35), calls=%async_computation.3 | async-start | bytes 262144 | tf_op jit(solution)/shard_map/all_to_all | solution.py:126
  82.0 73.9 %all-reduce.2.cloned.1.call-start = ((), (), s32[]{:S(2)}) async-start(), calls=%async_computation.6 | async-start | bytes 524288 | tf_op jit(solution)/shard_map/psum | solution.py:141
Sparse Core Ops, SparseCore 0:
  77.5 40.4 reduce-scatter.1
  120.4 35.5 all-reduce.1
where the time goes:
time: 165 us
  waiting for transfers between devices  78.2 us (47%)
  local copies, waits for them, and re-layouts  26.2 us (16%)
  matrix products  19.5 us (12%)
  starting transfers between devices  16.2 us (10%)
  between operations  14.3 us (9%)
  other arithmetic  7.41 us (4%)
  loops' own time  2.68 us (2%)
    psum x1, waiting for transfers between devices, per_device(): grads = lax.psum(band_rows, 'grp').astype(jnp.float32)  35.6 us
    reduce_scatter x1, waiting for transfers between devices, per_device(): lax.psum_scatter(term.astype(jnp.bfloat16), 'band', scatter_dimension=0,...  33.6 us
    dynamic_update_slice x8, local copies, waits for them, and re-layouts, band_attention(): stacked = lax.map(per_group, jnp.arange(groups))  5.51 us
    all_to_all x1, starting transfers between devices, per_device(): lax.all_to_all(send_bias, 'band', split_axis=0, concat_axis=0, tiled=True)  5.2 us
    all_to_all x1, waiting for transfers between devices, per_device(): lax.all_to_all(send_feat, 'band', split_axis=0, concat_axis=0, tiled=True)  5.13 us
    all_to_all x1, starting transfers between devices, per_device(): lax.all_to_all(send_mask, 'band', split_axis=0, concat_axis=0, tiled=True)  4.19 us
    dynamic_slice x8, local copies, waits for them, and re-layouts, per_group(): lax.dynamic_slice_in_dim(query, start, group_width, 1)  4.14 us
    dynamic_slice x8, local copies, waits for them, and re-layouts, per_group(): lax.dynamic_slice_in_dim(dattn, start, group_width, 1)  4.14 us
  transfers between devices with their start and end apart: 6, of which 4 were waited for; matrix products, arithmetic and copies ran while one was open for 8% of the time, Pallas kernels for 0%

commit v1 on v0

--- a/solution.py
+++ b/solution.py
@@ -138,7 +138,7 @@
         [grad_wq, grad_pair[:, :width], grad_pair[:, width:], grad_wo], axis=0
     ) / float(group_count)
     band_rows = lax.psum_scatter(term.astype(jnp.bfloat16), "band", scatter_dimension=0, tiled=True)
-    grads = lax.psum(band_rows, "grp").astype(jnp.float32)
+    grads = jnp.sum(lax.all_gather(band_rows, "grp"), axis=0).astype(jnp.float32)
     return (attended, grad_latent, grad_obs, grads)
 
 

time: 165 us -> 158 us (0.958)
  waiting for transfers between devices: 78.2 us -> 69.9 us
    psum x1 -> x0, waiting for transfers between devices: 35.6 us -> none  [per_device(): grads = lax.psum(band_rows, 'grp').astype(jnp.float32)]
    all_gather x0 -> x1, waiting for transfers between devices: none -> 18.5 us  [per_device(): lax.all_gather(band_rows, 'grp')]
    reduce_scatter x1, waiting for transfers between devices: 33.6 us -> 40.6 us  [per_device(): lax.psum_scatter(term.astype(jnp.bfloat16), 'band', scatter_dimension=0,...]
    all_to_all x1, waiting for transfers between devices: 0.01 us -> 1.84 us  [per_device(): lax.all_to_all(feat_grad.reshape(slots, OB * width), 'band', split_axis=0...]
  transfers between devices with their start and end apart: 6 -> 6, of which waited for: 4 -> 5; matrix products, arithmetic and copies ran while one was open for 8% -> 8% of each run, Pallas kernels for 0% -> 0%
where the time goes in v1:
time: 158 us; the launch traced here: 157 us
  waiting for transfers between devices  69.9 us (44%)
  local copies, waits for them, and re-layouts  26.2 us (17%)
  matrix products  19.5 us (12%)
  starting transfers between devices  16.2 us (10%)
  between operations  14.3 us (9%)
  other arithmetic  7.92 us (5%)
  loops' own time  2.68 us (2%)
    reduce_scatter x1, waiting for transfers between devices, per_device(): lax.psum_scatter(term.astype(jnp.bfloat16), 'band', scatter_dimension=0,...  40.6 us
    all_gather x1, waiting for transfers between devices, per_device(): lax.all_gather(band_rows, 'grp')  18.5 us
    dynamic_update_slice x8, local copies, waits for them, and re-layouts, band_attention(): stacked = lax.map(per_group, jnp.arange(groups))  5.51 us
    all_to_all x1, starting transfers between devices, per_device(): lax.all_to_all(send_bias, 'band', split_axis=0, concat_axis=0, tiled=True)  5.2 us
    all_to_all x1, waiting for transfers between devices, per_device(): lax.all_to_all(send_feat, 'band', split_axis=0, concat_axis=0, tiled=True)  5.13 us
    all_to_all x1, starting transfers between devices, per_device(): lax.all_to_all(send_mask, 'band', split_axis=0, concat_axis=0, tiled=True)  4.19 us
    dynamic_slice x8, local copies, waits for them, and re-layouts, per_group(): lax.dynamic_slice_in_dim(query, start, group_width, 1)  4.14 us
    dynamic_slice x8, local copies, waits for them, and re-layouts, per_group(): lax.dynamic_slice_in_dim(dattn, start, group_width, 1)  4.14 us
  transfers between devices with their start and end apart: 6, of which 5 were waited for; matrix products, arithmetic and copies ran while one was open for 8% of the time, Pallas kernels for 0%

profile of v1, /device:TPU:0, one launch (start us, length us, event | category | flops | bytes accessed | tf_op | source)
XLA Modules:
  0.0 156.8 jit_solution(9885838697826232023)
XLA Ops:
  7.2 0.9 convert_reduce_fusion
  8.1 0.7 multiply_add_fusion
  8.7 0.7 reshape.147
  9.7 0.7 copy.38
  10.3 5.2 %all-to-all-start.2 = ((bf16[8,2,8]{2,1,0:T(2,128)(2,1)}), bf16[8,2,8]{2,1,0:T(2,128)(2,1)S(1)}, u32[]{:S(2)}, u32[]{:S(2)}) async-start(bf16[8,2,8]{2,1,0:T(2,128)(2,1)} %bitcast.1), calls=%async_computation.2 | async-start | bytes 8192 | tf_op jit(solution)/shard_map/all_to_all | solution.py:99
  15.6 1.0 reshape.145
  16.8 1.1 constant_dynamic-update-slice_fusion.5
  17.9 0.8 convolution_convert_fusion.10
  18.7 1.1 constant_dynamic-update-slice_fusion.4
  19.8 1.2 convolution_convert_fusion.7
  21.1 1.3 convolution_convert_fusion.6
  22.3 0.7 copy.39
  23.0 4.2 %all-to-all-start.1 = ((bf16[8,2,8]{2,1,0:T(2,128)(2,1)}), bf16[8,2,8]{2,1,0:T(2,128)(2,1)S(1)}, u32[]{:S(2)}, u32[]{:S(2)}) async-start(bf16[8,2,8]{2,1,0:T(2,128)(2,1)} %bitcast.2), calls=%async_computation.1 | async-start | bytes 8192 | tf_op jit(solution)/shard_map/all_to_all | solution.py:100
  27.2 0.8 all_to_all.28
  28.1 3.8 %all-to-all-done.1 = bf16[8,2,8]{2,1,0:T(2,128)(2,1)S(1)} async-done(((bf16[8,2,8]{2,1,0:T(2,128)(2,1)}), bf16[8,2,8]{2,1,0:T(2,128)(2,1)S(1)}, u32[]{:S(2)}, u32[]{:S(2)}) %all-to-all-start.1) | async-done | bytes 288 | tf_op jit(solution)/shard_map/all_to_all | solution.py:100
  31.9 3.4 %all-to-all-start = ((bf16[8,2,4096]{2,1,0:T(2,128)(2,1)}), bf16[8,2,4096]{2,1,0:T(2,128)(2,1)S(1)}, u32[]{:S(2)}, u32[]{:S(2)}) async-start(bf16[8,2,4096]{2,1,0:T(2,128)(2,1)} %all_to_all.28), calls=%async_computation | async-start | bytes 262144 | tf_op jit(solution)/shard_map/all_to_all | solution.py:98
  35.6 5.1 %all-to-all-done = bf16[8,2,4096]{2,1,0:T(2,128)(2,1)S(1)} async-done(((bf16[8,2,4096]{2,1,0:T(2,128)(2,1)}), bf16[8,2,4096]{2,1,0:T(2,128)(2,1)S(1)}, u32[]{:S(2)}, u32[]{:S(2)}) %all-to-all-start) | async-done | bytes 131104 | tf_op jit(solution)/shard_map/all_to_all | solution.py:98
  41.1 30.6 %while.17 = (s32[]{:T(128)}, bf16[4,512,128]{1,2,0:T(8,128)(2,1)}, bf16[4,512,128]{1,2,0:T(8,128)(2,1)}, bf16[4,128,128]{1,2,0:T(8,128)(2,1)}, bf16[4,128,128]{1...) while((s32[]{:T(128)}, bf16[4,512,128]{1,2,0:T(8,128)(2,1)}, ...), condition=%wide.region_5.6_spmd.clone, body=%wide.region_1.5_spmd.clone.sunk | while | flops 107726848 | bytes 13525743 | solution.py:63
  41.2 0.6 dynamic_slice.34
  42.5 0.9 constant_dynamic-slice_fusion.9
  43.5 0.4 select_reduce_fusion.2
  44.2 0.9 constant_dynamic-slice_fusion.10
  45.4 0.5 multiply_reduce_fusion.2
  46.8 0.7 constant_dynamic-update-slice_fusion.8
  48.1 0.7 constant_dynamic-update-slice_fusion.9
  48.8 0.6 dynamic_slice.34
  50.1 0.9 constant_dynamic-slice_fusion.9
  51.2 0.4 select_reduce_fusion.2
  51.8 0.9 constant_dynamic-slice_fusion.10
  53.0 0.5 multiply_reduce_fusion.2
  54.0 0.4 convolution_convert_fusion.14
  54.4 0.7 constant_dynamic-update-slice_fusion.8
  55.8 0.7 constant_dynamic-update-slice_fusion.9
  56.5 0.6 dynamic_slice.34
  57.8 0.9 constant_dynamic-slice_fusion.9
  58.8 0.4 select_reduce_fusion.2
  59.5 0.9 constant_dynamic-slice_fusion.10
  60.7 0.5 multiply_reduce_fusion.2
  61.7 0.4 convolution_convert_fusion.14
  62.1 0.7 constant_dynamic-update-slice_fusion.8
  63.5 0.7 constant_dynamic-update-slice_fusion.9
  64.1 0.6 dynamic_slice.34
  65.4 0.9 constant_dynamic-slice_fusion.9
  66.5 0.4 select_reduce_fusion.2
  67.2 0.9 constant_dynamic-slice_fusion.10
  68.3 0.5 multiply_reduce_fusion.2
  69.7 0.7 constant_dynamic-update-slice_fusion.8
  71.1 0.7 constant_dynamic-update-slice_fusion.9
  71.8 1.5 fusion.27
  73.3 0.5 fusion.12
  74.0 0.8 copy-done.4
  75.0 0.5 convolution_bitcast_fusion
  75.5 1.9 %fusion.11 = bf16[2048,512]{1,0:T(8,128)(2,1)} fusion(f32[512,512]{1,0:T(8,128)S(1)} %fusion.27, f32[512,512]{1,0:T(8,128)S(1)} %get-tuple-element.169, f32[512,512]{1,0:T(8,128)S(1)} %get-tuple-element.168, f32[512,512]{1,0:T(8,128)S(1)} %convolution_bitcast_fusion), kind=kLoop, calls=%fused_computation.31 | loop fusion | flops 5242880 | bytes 6291456 | tf_op jit(solution)/shard_map/convert_element_type | solution.py:140
  77.5 40.6 %reduce-scatter.2.cloned.1.call-done = bf16[256,512]{1,0:T(8,128)(2,1)} async-done(((bf16[2048,512]{1,0:T(8,128)(2,1)}), bf16[256,512]{1,0:T(8,128)(2,1)}) %reduce-scatter.2.cloned.1.call-update) | async-done | bytes 262160 | tf_op jit(solution)/shard_map/reduce_scatter | solution.py:140
  118.0 0.5 convolution_convert_fusion.9
  118.5 0.7 all_to_all.35
  119.3 3.4 %all-to-all-start.3 = ((bf16[8,2,4096]{2,1,0:T(2,128)(2,1)}), bf16[8,2,4096]{2,1,0:T(2,128)(2,1)S(1)}, u32[]{:S(2)}, u32[]{:S(2)}) async-start(bf16[8,2,4096]{2,1,0:T(2,128)(2,1)} %all_to_all.35), calls=%async_computation.3 | async-start | bytes 262144 | tf_op jit(solution)/shard_map/all_to_all | solution.py:126
  122.7 2.3 %convolution_convert_fusion.5 = bf16[512,512]{1,0:T(8,128)(2,1)} fusion(bf16[512,512]{0,1:T(8,128)(2,1)} %bitcast.125, bf16[512,512]{1,0:T(8,128)(2,1)S(1)} %copy-done.7), kind=kOutput, calls=%fused_computation.34 | convolution fusion | flops 268697600 | bytes 1572864 | tf_op jit(solution)/shard_map/dot_general | solution.py:118
  125.0 1.3 convolution_convert_fusion.4
  126.3 1.8 %all-to-all-done.3 = bf16[8,2,4096]{2,1,0:T(2,128)(2,1)S(1)} async-done(((bf16[8,2,4096]{2,1,0:T(2,128)(2,1)}), bf16[8,2,4096]{2,1,0:T(2,128)(2,1)S(1)}, u32[]{:S(2)}, u32[]{:S(2)}) %all-to-all-start.3) | async-done | bytes 131104 | tf_op jit(solution)/shard_map/all_to_all | solution.py:126
  128.4 0.7 reshape.152
  129.1 18.5 %all-gather.3.cloned.1.call-done = bf16[1024,512]{1,0:T(8,128)(2,1)} async-done(((bf16[256,512]{1,0:T(8,128)(2,1)}), bf16[1024,512]{1,0:T(8,128)(2,1)}) %all-gather.3.cloned.1.call-update) | async-done | bytes 1048592 | tf_op jit(solution)/shard_map/all_gather | solution.py:141
  147.6 1.5 reduce_sum.40
  149.1 0.9 convert_element_type.137
  (98 shorter events, 10.3 us)
Async XLA Ops:
  7.2 13.9 %copy-start = (bf16[512,512]{1,0:T(8,128)(2,1)S(1)}, bf16[512,512]{1,0:T(8,128)(2,1)}, u32[]{:S(2)}) copy-start(bf16[512,512]{1,0:T(8,128)(2,1)} %param.21) | copy-start | bytes 1572868
  7.2 12.6 %copy-start.3 = (bf16[512,512]{1,0:T(8,128)(2,1)S(1)}, bf16[512,512]{1,0:T(8,128)(2,1)}, u32[]{:S(2)}) copy-start(bf16[512,512]{1,0:T(8,128)(2,1)} %param.12) | copy-start | bytes 1572868
  7.2 12.6 %copy-start.1 = (bf16[512,512]{1,0:T(8,128)(2,1)S(1)}, bf16[512,512]{1,0:T(8,128)(2,1)}, u32[]{:S(2)}) copy-start(bf16[512,512]{1,0:T(8,128)(2,1)} %param.17) | copy-start | bytes 1572868
  10.3 12.7 %all-to-all-start.2 = ((bf16[8,2,8]{2,1,0:T(2,128)(2,1)}), bf16[8,2,8]{2,1,0:T(2,128)(2,1)S(1)}, u32[]{:S(2)}, u32[]{:S(2)}) async-start(bf16[8,2,8]{2,1,0:T(2,128)(2,1)} %bitcast.1), calls=%async_computation.2 | async-start | bytes 8192 | tf_op jit(solution)/shard_map/all_to_all | solution.py:99
  15.6 5.5 %copy-start.6 = (bf16[512,512]{1,0:T(8,128)(2,1)S(1)}, bf16[512,512]{1,0:T(8,128)(2,1)}, u32[]{:S(2)}) copy-start(bf16[512,512]{1,0:T(8,128)(2,1)} %param.20) | copy-start | bytes 1572868
  23.0 8.9 %all-to-all-start.1 = ((bf16[8,2,8]{2,1,0:T(2,128)(2,1)}), bf16[8,2,8]{2,1,0:T(2,128)(2,1)S(1)}, u32[]{:S(2)}, u32[]{:S(2)}) async-start(bf16[8,2,8]{2,1,0:T(2,128)(2,1)} %bitcast.2), calls=%async_computation.1 | async-start | bytes 8192 | tf_op jit(solution)/shard_map/all_to_all | solution.py:100
  31.9 8.8 %all-to-all-start = ((bf16[8,2,4096]{2,1,0:T(2,128)(2,1)}), bf16[8,2,4096]{2,1,0:T(2,128)(2,1)S(1)}, u32[]{:S(2)}, u32[]{:S(2)}) async-start(bf16[8,2,4096]{2,1,0:T(2,128)(2,1)} %all_to_all.28), calls=%async_computation | async-start | bytes 262144 | tf_op jit(solution)/shard_map/all_to_all | solution.py:98
  35.3 82.8 %reduce-scatter.2.cloned.1.call-start = ((), (), s32[]{:S(2)}) async-start(), calls=%async_computation.5 | async-start | bytes 2359296 | tf_op jit(solution)/shard_map/reduce_scatter | solution.py:140
  71.8 1.5 copy-start.8
  71.8 1.5 copy-start.9
  73.8 1.0 copy-start.4
  73.8 1.2 copy-start.5
  77.4 45.3 %copy-start.7 = (bf16[512,512]{1,0:T(8,128)(2,1)S(1)}, bf16[512,512]{1,0:T(8,128)(2,1)}, u32[]{:S(2)}) copy-start(bf16[512,512]{1,0:T(8,128)(2,1)} %param.20) | copy-start | bytes 1572868
  77.4 47.6 %copy-start.2 = (bf16[512,512]{1,0:T(8,128)(2,1)S(1)}, bf16[512,512]{1,0:T(8,128)(2,1)}, u32[]{:S(2)}) copy-start(bf16[512,512]{1,0:T(8,128)(2,1)} %param.17) | copy-start | bytes 1572868
  77.4 70.2 %all-gather.3.cloned.1.call-start = ((), (), s32[]{:S(2)}) async-start(), calls=%async_computation.6 | async-start | bytes 1310720 | tf_op jit(solution)/shard_map/all_gather | solution.py:141
  119.3 8.8 %all-to-all-start.3 = ((bf16[8,2,4096]{2,1,0:T(2,128)(2,1)}), bf16[8,2,4096]{2,1,0:T(2,128)(2,1)S(1)}, u32[]{:S(2)}, u32[]{:S(2)}) async-start(bf16[8,2,4096]{2,1,0:T(2,128)(2,1)} %all_to_all.35), calls=%async_computation.3 | async-start | bytes 262144 | tf_op jit(solution)/shard_map/all_to_all | solution.py:126
Sparse Core Ops, SparseCore 0:
  77.5 40.4 reduce-scatter.1
  119.6 27.9 all-gather.2
